TPU v7x, 512 devices: a whole 4x8x8 slice. The times are simulated.
512 devices in a mesh: mode: 16 (over z_hi, x), mer: 32 (over y, z_lo, core).
Axes of the slice: x: 4, y: 8, z: 8 (z_hi: 4, z_lo: 2; z = z_hi * 2 + z_lo), core: 2. Of those that a mesh axis runs over, the one named last changes fastest.
Arguments:
- field: float32 [128, 6, 16384], P('mode', None, 'mer'), may hold values from -6 to 6
- velocity: bfloat16 [3, 256, 16384], P(None, None, ('mer', 'mode')), may hold values from -4 to 4
- stiffness: float32 [64, 64], replicated, may hold values from -0.75 to 0.75
- curl_matrix: float32 [64, 64], replicated, may hold values from -0.75 to 0.75
- mass: float32 [16384], P('mer'), may hold values from 0.5 to 2
- connect: int32 [512, 64], P('mer'), may hold values from 0 to 767
- wall_index: int32 [2048], P('mer'), may hold values from 0 to 511, as said below
- dtn: bfloat16 [128, 2048, 2048], P('mode', 'mer'), as said below
Outputs:
- advanced: float32 [128, 6, 16384], P('mode', None, 'mer')
- wall_flux: float32 [2, 128, 2, 2048], P(None, 'mode', None, 'mer')
Inputs may be any that keep to these rules, and one draw needn't show every extreme that they name: `wall_index`: within each block of 64 consecutive entries the numbers are distinct. `dtn`: each mode's matrix is symmetric.
All inputs are finite; a program needn't handle non-finite values.
Results may differ from a plain program's by a relative error of at most 0.005.
Values may be sent and summed in bfloat16 or wider, within the bound.
No kernel may reach another device: no remote copies, remote signals or barrier semaphores. Data moves between devices by JAX's collectives and lax.ppermute only.
A program may use at most 64 MiB of HBM per device.

v0:
```python
import jax
import jax.numpy as jnp
from jax import lax
from jax.sharding import PartitionSpec as P

GHOST = 256
HI = lax.Precision.HIGHEST


def from_behind(block, axis, distance):
    devices = range(lax.axis_size(axis))
    route = [(i - distance, i) for i in devices if i - distance in devices]
    return lax.ppermute(block, axis, route)


def tables(modes, nphi):
    m = jnp.arange(modes, dtype=jnp.float32)
    k = jnp.arange(nphi, dtype=jnp.float32)
    angle = 2.0 * jnp.pi * m[:, None] * k[None, :] / nphi
    forward = jnp.stack([jnp.cos(angle), -jnp.sin(angle)], 1)
    return (forward, forward / nphi)


def induced(moved, velocity):
    modes = moved.shape[0]
    nphi = velocity.shape[1]
    forward, inverse = tables(modes, nphi)
    phys = jnp.einsum("mpcn,mpk->ckn", moved.reshape(modes, 2, 3, -1), forward, precision=HI)
    vel = velocity.astype(jnp.float32)
    cross = jnp.stack(
        [
            vel[1] * phys[2] - vel[2] * phys[1],
            vel[2] * phys[0] - vel[0] * phys[2],
            vel[0] * phys[1] - vel[1] * phys[0],
        ]
    )
    back = jnp.einsum("ckn,mpk->mpcn", cross, inverse, precision=HI)
    return back.reshape(modes, 6, -1)


def split_pair(values):
    upper = values.astype(jnp.bfloat16)
    lower = (values - upper.astype(jnp.float32)).astype(jnp.bfloat16)
    return (upper, lower)


def element_sweep(extended, stiffness, curl_matrix, connect):
    mode_dev = extended.shape[0]
    ext_len = extended.shape[2]
    elem_dev = connect.shape[0]
    npe = connect.shape[1]
    per_block = min(elem_dev, max(1, 512 // npe))
    blocks = elem_dev // per_block
    rows = extended.reshape(mode_dev * 12, ext_len)
    rows_hi, rows_lo = split_pair(rows)
    indices = connect.reshape(blocks, per_block * npe)
    columns = jnp.arange(ext_len, dtype=jnp.int32)

    def step(summed, idx):
        onehot = (idx[:, None] == columns[None, :]).astype(jnp.bfloat16)
        picked = lax.dot_general(
            rows_hi, onehot, (((1,), (1,)), ((), ())), preferred_element_type=jnp.float32
        )
        picked = picked + lax.dot_general(
            rows_lo, onehot, (((1,), (1,)), ((), ())), preferred_element_type=jnp.float32
        )
        picked = picked.reshape(mode_dev, 12, per_block, npe)
        fvals = picked[:, :6]
        evals = picked[:, 6:].reshape(mode_dev, 2, 3, per_block, npe)
        evals = jnp.roll(evals, 1, axis=2).reshape(mode_dev, 6, per_block, npe)
        local = -1.0 * jnp.einsum("pq,maeq->maep", stiffness, fvals, precision=HI)
        local = local + jnp.einsum("pq,maeq->maep", curl_matrix, evals, precision=HI)
        flat = local.reshape(mode_dev * 6, per_block * npe)
        loc_hi, loc_lo = split_pair(flat)
        summed = summed + jnp.dot(loc_hi, onehot, preferred_element_type=jnp.float32)
        summed = summed + jnp.dot(loc_lo, onehot, preferred_element_type=jnp.float32)
        return (summed, None)

    start = jnp.zeros((mode_dev * 6, ext_len), jnp.float32)
    summed, unused = lax.scan(step, start, indices)
    return summed.reshape(mode_dev, 6, ext_len)


def rate(field, velocity, stiffness, curl_matrix, mass, connect, wall_index, dtn):
    mode_dev = field.shape[0]
    nodes_dev = field.shape[2]
    extra = GHOST
    field_far = from_behind(field[:, :, :extra], "mer", -1)
    moved = lax.all_to_all(field, "mode", split_axis=2, concat_axis=0, tiled=True)
    back = induced(moved, velocity)
    emf = lax.all_to_all(back, "mode", split_axis=0, concat_axis=2, tiled=True)
    emf_far = from_behind(emf[:, :, :extra], "mer", -1)
    far = jnp.concatenate([field_far, emf_far], 1)
    extended = jnp.concatenate([jnp.concatenate([field, emf], 1), far], 2)
    summed = element_sweep(extended, stiffness, curl_matrix, connect)
    incoming = from_behind(summed[:, :, nodes_dev:], "mer", 1)
    assembled = summed[:, :, :nodes_dev].at[:, :, :extra].add(incoming)
    trace = field[:, jnp.array([2, 5])][:, :, wall_index].astype(jnp.bfloat16)
    whole = lax.all_gather(trace, "mer", axis=2, tiled=True)
    flux = jnp.einsum("mwv,mpv->mpw", dtn, whole, preferred_element_type=jnp.float32)
    mode_num = lax.axis_index("mode") * mode_dev + jnp.arange(mode_dev, dtype=jnp.int32)
    coef = (mode_num.astype(jnp.float32) / all_modes(velocity)) ** 2
    total = assembled - 4.0 * coef[:, None, None] * mass[None, None, :] * field
    total = total.at[:, 2, wall_index].add(-0.5 * flux[:, 0])
    total = total.at[:, 5, wall_index].add(-0.5 * flux[:, 1])
    return (total / mass[None, None, :], flux)


def all_modes(velocity):
    return velocity.shape[1] // 2


def body(field, velocity, stiffness, curl_matrix, mass, connect, wall_index, dtn):
    args = (velocity, stiffness, curl_matrix, mass, connect, wall_index, dtn)
    first, flux_one = rate(field, *args)
    section = field + 0.2 * first
    second, flux_two = rate(section, *args)
    return (0.5 * (field + section + 0.2 * second), jnp.stack([flux_one, flux_two]))


def solution(mesh):
    placed = (
        P("mode", None, "mer"),
        P(None, None, ("mer", "mode")),
        P(),
        P(),
        P("mer"),
        P("mer", None),
        P("mer"),
        P("mode", "mer", None),
    )
    return jax.shard_map(
        body,
        mesh=mesh,
        in_specs=placed,
        out_specs=(P("mode", None, "mer"), P(None, "mode", None, "mer")),
        check_vma=False,
    )
```

profile of v0, /device:TPU:32, one launch (start us, length us, event | category | flops | bytes accessed | tf_op | source)
XLA Modules:
  0.0 253.3 jit_solution(7026488388729421583)
XLA Ops:
  0.6 3.0 %copy.153 = f32[8,6,512]{0,1,2:T(8,128)} copy(f32[8,6,512]{2,0,1:T(8,128)} %param.18) | data formatting | bytes 196608 | tf_op args[0]
  3.6 2.9 %reshape.321 = f32[16,1,1536]{2,1,0:T(1,128)} reshape(f32[512,6,8]{2,1,0:T(8,128)} %bitcast.196) | data formatting | bytes 196608
  6.6 12.9 %all-to-all-start = ((f32[16,1,1536]{2,1,0:T(1,128)}), f32[16,1,1536]{2,1,0:T(1,128)}, u32[]{:S(2)}, u32[]{:S(2)}) async-start(f32[16,1,1536]{2,1,0:T(1,128)} %reshape.321), calls=%async_computation | async-start | bytes 196608 | tf_op jit(solution)/shard_map/all_to_all | solution.py:89
  20.1 2.4 collective-permute-start
  25.2 34.2 %all_gather.6 = bf16[8,2,2048]{0,1,2:T(2,128)(2,1)S(1)} all-gather(bf16[8,2,64]{0,1,2:T(2,128)(2,1)S(1)} %bitcast.215), channel_id=1, replica_groups=mesh['mode'=16,'mer'=32] {'mer'}, dimensions={2}, use_global_device_ids=true | all-gather | bytes 67584 | tf_op jit(solution)/shard_map/all_gather | solution.py:99
  63.6 2.2 reshape.322
  70.2 9.6 %all-to-all-start.1 = ((f32[16,1,1536]{2,1,0:T(1,128)}), f32[16,1,1536]{2,1,0:T(1,128)S(1)}, u32[]{:S(2)}, u32[]{:S(2)}) async-start(f32[16,1,1536]{2,1,0:T(1,128)} %reshape.323), calls=%async_computation.1 | async-start | bytes 196608 | tf_op jit(solution)/shard_map/all_to_all | solution.py:91
  79.9 10.3 %all-to-all-done.1 = f32[16,1,1536]{2,1,0:T(1,128)S(1)} async-done(((f32[16,1,1536]{2,1,0:T(1,128)}), f32[16,1,1536]{2,1,0:T(1,128)S(1)}, u32[]{:S(2)}, u32[]{:S(2)}) %all-to-all-start.1) | async-done | bytes 98336 | tf_op jit(solution)/shard_map/all_to_all | solution.py:91
  98.7 10.9 %while.24 = (s32[]{:T(128)}, f32[48,768]{1,0:T(8,128)}, s32[2,512]{1,0:T(2,128)S(1)}, bf16[96,768]{1,0:T(8,128)(2,1)}, bf16[96,768]{1,0:T(8,128)(2,1)}, /*index=...) while((s32[]{:T(128)}, f32[48,768]{1,0:T(8,128)}, s32[2,512]{1,0:T(2,128)S(1)}, ...), condition=%wide.region_1.2_spmd.clone, body=%wide.region_0.1_spmd.clone.sunk | while | flops 266170368 | bytes 4665507 | solution.py:80
  110.6 3.0 %collective-permute-start.2 = (f32[8,6,256]{2,0,1:T(8,128)S(1)}, f32[8,6,256]{2,0,1:T(8,128)S(1)}, u32[]{:S(2)}, u32[]{:S(2)}) collective-permute-start(f32[8,6,256]{2,0,1:T(8,128)S(1)} %copy.162), channel_id=1, source_target_pairs={{0,1},{1,2},{2,3},{3,4},{4,5},{5,6},{6,7},{7,8},{8,9},{9,10},{10,1... | collective-permute-start | bytes 147464 | tf_op jit(solution)/shard_map/ppermute | solution.py:13
  113.8 4.3 %collective-permute-done.2 = f32[8,6,256]{2,0,1:T(8,128)S(1)} collective-permute-done((f32[8,6,256]{2,0,1:T(8,128)S(1)}, f32[8,6,256]{2,0,1:T(8,128)S(1)}, u32[]{:S(2)}, u32[]{:S(2)}) %collective-permute-start.2) | collective-permute-done | bytes 49184 | tf_op jit(solution)/shard_map/ppermute | solution.py:13
  119.8 7.0 %scatter_fusion = f32[8,6,512]{0,2,1:T(8,128)} fusion(f32[8,6,512]{0,2,1:T(8,128)} %copy.165, s32[64]{0:T(128)S(1)} %select_bitcast_fusion.1, f32[64,8]{1,0:T(8,128)S(1)} %copy.166), kind=kCustom, calls=%fused_computation.4 | custom fusion | flops 512 | bytes 6656 | tf_op jit(solution)/shard_map/scatter-add | solution.py:104
  126.9 7.0 %scatter_fusion.1 = f32[8,6,512]{0,2,1:T(8,128)} fusion(f32[8,6,512]{0,2,1:T(8,128)} %scatter_fusion, s32[64]{0:T(128)S(1)} %get-tuple-element.204, f32[64,8]{1,0:T(8,128)S(1)} %copy.167), kind=kCustom, calls=%fused_computation.5 | custom fusion | flops 512 | bytes 6656 | tf_op jit(solution)/shard_map/scatter-add | solution.py:105
  137.7 2.9 %reshape.325 = f32[16,1,1536]{2,1,0:T(1,128)} reshape(f32[512,6,8]{2,1,0:T(8,128)} %bitcast.197) | data formatting | bytes 196608
  140.6 4.2 %all-to-all-start.2 = ((f32[16,1,1536]{2,1,0:T(1,128)}), f32[16,1,1536]{2,1,0:T(1,128)}, u32[]{:S(2)}, u32[]{:S(2)}) async-start(f32[16,1,1536]{2,1,0:T(1,128)} %reshape.325), calls=%async_computation.2 | async-start | bytes 196608 | tf_op jit(solution)/shard_map/all_to_all | solution.py:89
  149.4 33.9 %all_gather.7 = bf16[8,2,2048]{0,1,2:T(2,128)(2,1)S(1)} all-gather(bf16[8,2,64]{0,1,2:T(2,128)(2,1)} %bitcast.214), channel_id=1, replica_groups=mesh['mode'=16,'mer'=32] {'mer'}, dimensions={2}, use_global_device_ids=true | all-gather | bytes 67584 | tf_op jit(solution)/shard_map/all_gather | solution.py:99
  186.8 2.2 reshape.326
  193.4 9.5 %all-to-all-start.3 = ((f32[16,1,1536]{2,1,0:T(1,128)}), f32[16,1,1536]{2,1,0:T(1,128)S(1)}, u32[]{:S(2)}, u32[]{:S(2)}) async-start(f32[16,1,1536]{2,1,0:T(1,128)} %reshape.327), calls=%async_computation.3 | async-start | bytes 196608 | tf_op jit(solution)/shard_map/all_to_all | solution.py:91
  203.5 10.0 %all-to-all-done.3 = f32[16,1,1536]{2,1,0:T(1,128)S(1)} async-done(((f32[16,1,1536]{2,1,0:T(1,128)}), f32[16,1,1536]{2,1,0:T(1,128)S(1)}, u32[]{:S(2)}, u32[]{:S(2)}) %all-to-all-start.3) | async-done | bytes 98336 | tf_op jit(solution)/shard_map/all_to_all | solution.py:91
  219.6 7.7 %while.25 = (s32[]{:T(128)}, f32[48,768]{1,0:T(8,128)S(1)}, s32[2,512]{1,0:T(2,128)S(1)}, bf16[96,768]{1,0:T(8,128)(2,1)}, bf16[96,768]{1,0:T(8,128)(2,1)S(1)}, ...) while((s32[]{:T(128)}, f32[48,768]{1,0:T(8,128)S(1)}, ...), condition=%wide.region_5.6_spmd.clone, body=%wide.region_4.5_spmd.clone.sunk | while | flops 266170368 | bytes 3485803 | solution.py:80
  227.5 3.2 %collective-permute-start.5 = (f32[8,6,256]{2,0,1:T(8,128)S(1)}, f32[8,6,256]{2,0,1:T(8,128)S(1)}, u32[]{:S(2)}, u32[]{:S(2)}) collective-permute-start(f32[8,6,256]{2,0,1:T(8,128)S(1)} %copy.178), channel_id=1, source_target_pairs={{0,1},{1,2},{2,3},{3,4},{4,5},{5,6},{6,7},{7,8},{8,9},{9,10},{10,1... | collective-permute-start | bytes 147464 | tf_op jit(solution)/shard_map/ppermute | solution.py:13
  231.5 3.5 %collective-permute-done.5 = f32[8,6,256]{2,0,1:T(8,128)S(1)} collective-permute-done((f32[8,6,256]{2,0,1:T(8,128)S(1)}, f32[8,6,256]{2,0,1:T(8,128)S(1)}, u32[]{:S(2)}, u32[]{:S(2)}) %collective-permute-start.5) | collective-permute-done | bytes 49184 | tf_op jit(solution)/shard_map/ppermute | solution.py:13
  236.7 7.0 %scatter_fusion.2 = f32[8,6,512]{0,2,1:T(8,128)} fusion(f32[8,6,512]{0,2,1:T(8,128)} %copy.181, s32[64]{0:T(128)S(1)} %select_bitcast_fusion.1, f32[64,8]{1,0:T(8,128)S(1)} %copy.182), kind=kCustom, calls=%fused_computation.6 | custom fusion | flops 512 | bytes 6656 | tf_op jit(solution)/shard_map/scatter-add | solution.py:104
  243.8 7.0 %scatter_fusion.3 = f32[8,6,512]{0,2,1:T(8,128)} fusion(f32[8,6,512]{0,2,1:T(8,128)} %scatter_fusion.2, s32[64]{0:T(128)S(1)} %get-tuple-element.204, f32[64,8]{1,0:T(8,128)S(1)} %copy.183), kind=kCustom, calls=%fused_computation.7 | custom fusion | flops 512 | bytes 6656 | tf_op jit(solution)/shard_map/scatter-add | solution.py:105
  (200 shorter events, 69.4 us)
Async XLA Ops:
  0.6 59.4 %copy-start = (bf16[8,64,2048]{2,1,0:T(8,128)(2,1)S(1)}, bf16[8,64,2048]{2,1,0:T(8,128)(2,1)}, u32[]{:S(2)}) copy-start(bf16[8,64,2048]{2,1,0:T(8,128)(2,1)} %param.25) | copy-start | bytes 6291460
  3.6 15.9 %copy-start.3 = (f32[8,6,512]{2,0,1:T(8,128)S(1)}, f32[8,6,512]{2,0,1:T(8,128)}, u32[]{:S(2)}) copy-start(f32[8,6,512]{2,0,1:T(8,128)} %param.18) | copy-start | bytes 294916
  3.6 19.0 %copy-start.14 = (bf16[3,256,32]{1,2,0:T(8,128)(2,1)S(1)}, bf16[3,256,32]{1,2,0:T(8,128)(2,1)}, u32[]{:S(2)}) copy-start(bf16[3,256,32]{1,2,0:T(8,128)(2,1)} %param.19) | copy-start | bytes 147460
  3.6 19.6 %copy-start.24 = (s32[64]{0:T(128)S(1)}, s32[64]{0:T(128)}, u32[]{:S(2)}) copy-start(s32[64]{0:T(128)} %param.24) | copy-start | bytes 772
  3.6 20.1 %copy-start.23 = (s32[2]{0:T(128)S(1)}, s32[2]{0:T(128)}, u32[]{:S(2)}) copy-start(s32[2]{0:T(128)} %constant.185) | copy-start | bytes 28
  6.6 54.7 %all-to-all-start = ((f32[16,1,1536]{2,1,0:T(1,128)}), f32[16,1,1536]{2,1,0:T(1,128)}, u32[]{:S(2)}, u32[]{:S(2)}) async-start(f32[16,1,1536]{2,1,0:T(1,128)} %reshape.321), calls=%async_computation | async-start | bytes 196608 | tf_op jit(solution)/shard_map/all_to_all | solution.py:89
  20.1 75.2 %collective-permute-start = (f32[8,6,256]{2,0,1:T(8,128)}, f32[8,6,256]{2,0,1:T(8,128)}, u32[]{:S(2)}, u32[]{:S(2)}) collective-permute-start(f32[8,6,256]{2,0,1:T(8,128)} %slice.160), channel_id=1, source_target_pairs={{1,0},{2,1},{3,2},{4,3},{5,4},{6,5},{7,6},{8,7},{9,8},{10,9},{11,1... | collective-permute-start | bytes 147464 | tf_op jit(solution)/shard_map/ppermute | solution.py:13
  22.6 46.0 %copy-start.8 = (f32[3,256,32]{1,2,0:T(8,128)}, f32[3,256,32]{1,2,0:T(8,128)S(1)}, u32[]{:S(2)}) copy-start(f32[3,256,32]{1,2,0:T(8,128)S(1)} %convert_element_type.56) | copy-start | bytes 294916
  60.7 34.6 %copy-start.15 = (f32[8,2,64]{2,1,0:T(2,128)}, f32[8,2,64]{2,1,0:T(2,128)S(1)}, u32[]{:S(2)}) copy-start(f32[8,2,64]{2,1,0:T(2,128)S(1)} %fusion.69) | copy-start | bytes 12292
  67.8 12.0 %copy-start.17 = (f32[512]{0:T(512)S(1)}, f32[512]{0:T(512)}, u32[]{:S(2)}) copy-start(f32[512]{0:T(512)} %param.22) | copy-start | bytes 6148
  67.8 12.0 %copy-start.22 = (f32[8]{0:T(128)S(1)}, f32[8]{0:T(128)}, u32[]{:S(2)}) copy-start(f32[8]{0:T(128)} %multiply_multiply_fusion.1) | copy-start | bytes 100
  69.3 26.0 %copy-start.18 = (s32[16,64]{1,0:T(8,128)S(1)}, s32[16,64]{1,0:T(8,128)}, u32[]{:S(2)}) copy-start(s32[16,64]{1,0:T(8,128)} %param.23) | copy-start | bytes 12292
  69.3 27.7 %copy-start.4 = (f32[8,6,512]{2,0,1:T(8,128)S(1)}, f32[8,6,512]{2,0,1:T(8,128)}, u32[]{:S(2)}) copy-start(f32[8,6,512]{2,0,1:T(8,128)} %param.18) | copy-start | bytes 294916
  70.2 20.0 %all-to-all-start.1 = ((f32[16,1,1536]{2,1,0:T(1,128)}), f32[16,1,1536]{2,1,0:T(1,128)S(1)}, u32[]{:S(2)}, u32[]{:S(2)}) async-start(f32[16,1,1536]{2,1,0:T(1,128)} %reshape.323), calls=%async_computation.1 | async-start | bytes 196608 | tf_op jit(solution)/shard_map/all_to_all | solution.py:91
  93.3 3.7 %collective-permute-start.1 = (f32[8,6,256]{2,0,1:T(8,128)S(1)}, f32[8,6,256]{2,0,1:T(8,128)S(1)}, u32[]{:S(2)}, u32[]{:S(2)}) collective-permute-start(f32[8,6,256]{2,0,1:T(8,128)S(1)} %slice.213), channel_id=1, source_target_pairs={{1,0},{2,1},{3,2},{4,3},{5,4},{6,5},{7,6},{8,7},{9,8},{10,9},{11,1... | collective-permute-start | bytes 147464 | tf_op jit(solution)/shard_map/ppermute | solution.py:13
  98.7 14.9 %copy-start.21 = (s32[64]{0:T(128)S(1)}, s32[64]{0:T(128)}, u32[]{:S(2)}) copy-start(s32[64]{0:T(128)} %copy-done.20) | copy-start | bytes 772
  110.6 7.6 %collective-permute-start.2 = (f32[8,6,256]{2,0,1:T(8,128)S(1)}, f32[8,6,256]{2,0,1:T(8,128)S(1)}, u32[]{:S(2)}, u32[]{:S(2)}) collective-permute-start(f32[8,6,256]{2,0,1:T(8,128)S(1)} %copy.162), channel_id=1, source_target_pairs={{0,1},{1,2},{2,3},{3,4},{4,5},{5,6},{6,7},{7,8},{8,9},{9,10},{10,1... | collective-permute-start | bytes 147464 | tf_op jit(solution)/shard_map/ppermute | solution.py:13
  140.6 44.4 %all-to-all-start.2 = ((f32[16,1,1536]{2,1,0:T(1,128)}), f32[16,1,1536]{2,1,0:T(1,128)}, u32[]{:S(2)}, u32[]{:S(2)}) async-start(f32[16,1,1536]{2,1,0:T(1,128)} %reshape.325), calls=%async_computation.2 | async-start | bytes 196608 | tf_op jit(solution)/shard_map/all_to_all | solution.py:89
  145.9 71.1 %collective-permute-start.3 = (f32[8,6,256]{2,0,1:T(8,128)}, f32[8,6,256]{2,0,1:T(8,128)S(1)}, u32[]{:S(2)}, u32[]{:S(2)}) collective-permute-start(f32[8,6,256]{2,0,1:T(8,128)} %slice.222), channel_id=1, source_target_pairs={{1,0},{2,1},{3,2},{4,3},{5,4},{6,5},{7,6},{8,7},{9,8},{10,9},{11,1... | collective-permute-start | bytes 147464 | tf_op jit(solution)/shard_map/ppermute | solution.py:13
  193.4 20.1 %all-to-all-start.3 = ((f32[16,1,1536]{2,1,0:T(1,128)}), f32[16,1,1536]{2,1,0:T(1,128)S(1)}, u32[]{:S(2)}, u32[]{:S(2)}) async-start(f32[16,1,1536]{2,1,0:T(1,128)} %reshape.327), calls=%async_computation.3 | async-start | bytes 196608 | tf_op jit(solution)/shard_map/all_to_all | solution.py:91
  203.5 15.2 %copy-start.7 = (f32[8,6,512]{2,0,1:T(8,128)S(1)}, f32[8,6,512]{2,0,1:T(8,128)}, u32[]{:S(2)}) copy-start(f32[8,6,512]{2,0,1:T(8,128)} %copy-done.6) | copy-start | bytes 294916
  215.0 3.8 %collective-permute-start.4 = (f32[8,6,256]{2,0,1:T(8,128)S(1)}, f32[8,6,256]{2,0,1:T(8,128)S(1)}, u32[]{:S(2)}, u32[]{:S(2)}) collective-permute-start(f32[8,6,256]{2,0,1:T(8,128)S(1)} %slice.223), channel_id=1, source_target_pairs={{1,0},{2,1},{3,2},{4,3},{5,4},{6,5},{7,6},{8,7},{9,8},{10,9},{11,1... | collective-permute-start | bytes 147464 | tf_op jit(solution)/shard_map/ppermute | solution.py:13
  227.5 7.6 %collective-permute-start.5 = (f32[8,6,256]{2,0,1:T(8,128)S(1)}, f32[8,6,256]{2,0,1:T(8,128)S(1)}, u32[]{:S(2)}, u32[]{:S(2)}) collective-permute-start(f32[8,6,256]{2,0,1:T(8,128)S(1)} %copy.178), channel_id=1, source_target_pairs={{0,1},{1,2},{2,3},{3,4},{4,5},{5,6},{6,7},{7,8},{8,9},{9,10},{10,1... | collective-permute-start | bytes 147464 | tf_op jit(solution)/shard_map/ppermute | solution.py:13
  235.1 17.5 %copy-start.5 = (f32[8,6,512]{2,0,1:T(8,128)S(1)}, f32[8,6,512]{2,0,1:T(8,128)}, u32[]{:S(2)}) copy-start(f32[8,6,512]{2,0,1:T(8,128)} %param.18) | copy-start | bytes 294916
  (13 other events, 59.0 us)
where the time goes:
time: 255 us; the launch traced here: 253 us
  blocking collectives  68.1 us (27%)
  starting transfers between devices  50.6 us (20%)
  local copies, waits for them, and re-layouts  43.8 us (17%)
  other arithmetic  38.3 us (15%)
  waiting for transfers between devices  31.3 us (12%)
  matrix products  19.4 us (8%)
    all_gather x2, blocking collectives, rate(): whole = lax.all_gather(trace, 'mer', axis=2, tiled=True)  68.1 us
    all_to_all x2, waiting for transfers between devices, rate(): emf = lax.all_to_all(back, 'mode', split_axis=0, concat_axis=2, tiled=True)  20.2 us
    all_to_all x2, starting transfers between devices, rate(): emf = lax.all_to_all(back, 'mode', split_axis=0, concat_axis=2, tiled=True)  19.1 us
    all_to_all x2, starting transfers between devices, rate(): lax.all_to_all(field, 'mode', split_axis=2, concat_axis=0, tiled=True)  17.1 us
    unnamed x57, local copies, waits for them, and re-layouts  16 us
    ppermute x6, starting transfers between devices, from_behind(): return lax.ppermute(block, axis, route)  14.5 us
    scatter-add x2, other arithmetic, rate(): total = total.at[:, 2, wall_index].add(-0.5 * flux[:, 0])  14.1 us
    scatter-add x2, other arithmetic, rate(): total = total.at[:, 5, wall_index].add(-0.5 * flux[:, 1])  13.9 us
  transfers between devices with their start and end apart: 10, of which 6 were waited for; matrix products, arithmetic and copies ran while one was open for 12% of the time, Pallas kernels for 0%

commit v1 on v0

--- a/solution.py
+++ b/solution.py
@@ -88,7 +88,10 @@
     field_far = from_behind(field[:, :, :extra], "mer", -1)
     moved = lax.all_to_all(field, "mode", split_axis=2, concat_axis=0, tiled=True)
     back = induced(moved, velocity)
-    emf = lax.all_to_all(back, "mode", split_axis=0, concat_axis=2, tiled=True)
+    emf = jnp.concatenate(
+        lax.all_to_all(jnp.stack(jnp.split(back, lax.axis_size("mode"), axis=0)), "mode", 0, 0),
+        axis=2,
+    )
     emf_far = from_behind(emf[:, :, :extra], "mer", -1)
     far = jnp.concatenate([field_far, emf_far], 1)
     extended = jnp.concatenate([jnp.concatenate([field, emf], 1), far], 2)

time: 255 us -> 292 us (1.15)
  local copies, waits for them, and re-layouts: 43.8 us -> 75.8 us
    another operation x2 -> x36, local copies, waits for them, and re-layouts: 0.02 us -> 23.1 us  [the longest x34 23 us: rate(): jnp.stack(jnp.split(back, lax.axis_size('mode'), axis=0))]
    unnamed x57 -> x89, local copies, waits for them, and re-layouts: 16 us -> 25.2 us
  transfers between devices with their start and end apart: 10 -> 10, of which waited for: 6 -> 6; matrix products, arithmetic and copies ran while one was open for 12% -> 23% of each run, Pallas kernels for 0% -> 0%
where the time goes in v1:
time: 292 us; the launch traced here: 289 us
  local copies, waits for them, and re-layouts  75.8 us (26%)
  blocking collectives  68 us (23%)
  starting transfers between devices  50.6 us (17%)
  other arithmetic  40.6 us (14%)
  waiting for transfers between devices  29.9 us (10%)
  matrix products  22.1 us (8%)
    all_gather x2, blocking collectives, rate(): whole = lax.all_gather(trace, 'mer', axis=2, tiled=True)  68 us
    unnamed x89, local copies, waits for them, and re-layouts  25.2 us
    another operation x34, local copies, waits for them, and re-layouts, rate(): jnp.stack(jnp.split(back, lax.axis_size('mode'), axis=0))  23 us
    all_to_all x2, starting transfers between devices, rate(): lax.all_to_all(jnp.stack(jnp.split(back, lax.axis_size('mode'), axis=0)),...  19.1 us
    all_to_all x2, waiting for transfers between devices, rate(): lax.all_to_all(jnp.stack(jnp.split(back, lax.axis_size('mode'), axis=0)),...  18.8 us
    all_to_all x2, starting transfers between devices, rate(): lax.all_to_all(field, 'mode', split_axis=2, concat_axis=0, tiled=True)  17.1 us
    ppermute x6, starting transfers between devices, from_behind(): return lax.ppermute(block, axis, route)  14.4 us
    scatter-add x2, other arithmetic, rate(): total = total.at[:, 5, wall_index].add(-0.5 * flux[:, 1])  14.1 us
  transfers between devices with their start and end apart: 10, of which 6 were waited for; matrix products, arithmetic and copies ran while one was open for 23% of the time, Pallas kernels for 0%

profile of v1, /device:TPU:32, one launch (start us, length us, event | category | flops | bytes accessed | tf_op | source)
XLA Modules:
  0.0 288.7 jit_solution(10159857579712655333)
XLA Ops:
  0.6 3.0 %copy.205 = f32[8,6,512]{0,1,2:T(8,128)} copy(f32[8,6,512]{2,0,1:T(8,128)} %param.18) | data formatting | bytes 196608 | tf_op args[0]
  3.7 2.9 %reshape.395 = f32[16,1,1536]{2,1,0:T(1,128)} reshape(f32[512,6,8]{2,1,0:T(8,128)} %bitcast.230) | data formatting | bytes 196608
  6.6 12.9 %all-to-all-start = ((f32[16,1,1536]{2,1,0:T(1,128)}), f32[16,1,1536]{2,1,0:T(1,128)}, u32[]{:S(2)}, u32[]{:S(2)}) async-start(f32[16,1,1536]{2,1,0:T(1,128)} %reshape.395), calls=%async_computation | async-start | bytes 196608 | tf_op jit(solution)/shard_map/all_to_all | solution.py:89
  20.2 2.4 collective-permute-start
  25.1 34.2 %all_gather.6 = bf16[8,2,2048]{0,1,2:T(2,128)(2,1)S(1)} all-gather(bf16[8,2,64]{0,1,2:T(2,128)(2,1)S(1)} %bitcast.279), channel_id=1, replica_groups=mesh['mode'=16,'mer'=32] {'mer'}, dimensions={2}, use_global_device_ids=true | all-gather | bytes 67584 | tf_op jit(solution)/shard_map/all_gather | solution.py:102
  63.7 2.2 reshape.396
  91.0 9.7 %all-to-all-start.1 = ((f32[16,1,1536]{2,1,0:T(1,128)}), f32[16,1,1536]{2,1,0:T(1,128)S(1)}, u32[]{:S(2)}, u32[]{:S(2)}) async-start(f32[16,1,1536]{2,1,0:T(1,128)} %reshape.397), calls=%async_computation.1 | async-start | bytes 196608 | tf_op jit(solution)/shard_map/all_to_all | solution.py:92
  101.4 9.7 %all-to-all-done.1 = f32[16,1,1536]{2,1,0:T(1,128)S(1)} async-done(((f32[16,1,1536]{2,1,0:T(1,128)}), f32[16,1,1536]{2,1,0:T(1,128)S(1)}, u32[]{:S(2)}, u32[]{:S(2)}) %all-to-all-start.1) | async-done | bytes 98336 | tf_op jit(solution)/shard_map/all_to_all | solution.py:92
  118.0 10.9 %while.24 = (s32[]{:T(128)}, f32[48,768]{1,0:T(8,128)}, s32[2,512]{1,0:T(2,128)S(1)}, bf16[96,768]{1,0:T(8,128)(2,1)}, bf16[96,768]{1,0:T(8,128)(2,1)}, /*index=...) while((s32[]{:T(128)}, f32[48,768]{1,0:T(8,128)}, s32[2,512]{1,0:T(2,128)S(1)}, ...), condition=%wide.region_1.2_spmd.clone, body=%wide.region_0.1_spmd.clone.sunk | while | flops 266170368 | bytes 4665507 | solution.py:80
  129.8 3.0 %collective-permute-start.2 = (f32[8,6,256]{2,0,1:T(8,128)S(1)}, f32[8,6,256]{2,0,1:T(8,128)S(1)}, u32[]{:S(2)}, u32[]{:S(2)}) collective-permute-start(f32[8,6,256]{2,0,1:T(8,128)S(1)} %copy.228), channel_id=1, source_target_pairs={{0,1},{1,2},{2,3},{3,4},{4,5},{5,6},{6,7},{7,8},{8,9},{9,10},{10,1... | collective-permute-start | bytes 147464 | tf_op jit(solution)/shard_map/ppermute | solution.py:13
  133.1 4.3 %collective-permute-done.2 = f32[8,6,256]{2,0,1:T(8,128)S(1)} collective-permute-done((f32[8,6,256]{2,0,1:T(8,128)S(1)}, f32[8,6,256]{2,0,1:T(8,128)S(1)}, u32[]{:S(2)}, u32[]{:S(2)}) %collective-permute-start.2) | collective-permute-done | bytes 49184 | tf_op jit(solution)/shard_map/ppermute | solution.py:13
  139.1 7.0 %scatter_fusion = f32[8,6,512]{0,2,1:T(8,128)} fusion(f32[8,6,512]{0,2,1:T(8,128)} %copy.231, s32[64]{0:T(128)S(1)} %select_bitcast_fusion.1, f32[64,8]{1,0:T(8,128)S(1)} %copy.232), kind=kCustom, calls=%fused_computation.4 | custom fusion | flops 512 | bytes 6656 | tf_op jit(solution)/shard_map/scatter-add | solution.py:107
  146.1 7.0 %scatter_fusion.1 = f32[8,6,512]{0,2,1:T(8,128)} fusion(f32[8,6,512]{0,2,1:T(8,128)} %scatter_fusion, s32[64]{0:T(128)S(1)} %get-tuple-element.204, f32[64,8]{1,0:T(8,128)S(1)} %copy.233), kind=kCustom, calls=%fused_computation.5 | custom fusion | flops 512 | bytes 6656 | tf_op jit(solution)/shard_map/scatter-add | solution.py:108
  157.0 2.9 %reshape.399 = f32[16,1,1536]{2,1,0:T(1,128)} reshape(f32[512,6,8]{2,1,0:T(8,128)} %bitcast.231) | data formatting | bytes 196608
  159.9 4.2 %all-to-all-start.2 = ((f32[16,1,1536]{2,1,0:T(1,128)}), f32[16,1,1536]{2,1,0:T(1,128)}, u32[]{:S(2)}, u32[]{:S(2)}) async-start(f32[16,1,1536]{2,1,0:T(1,128)} %reshape.399), calls=%async_computation.2 | async-start | bytes 196608 | tf_op jit(solution)/shard_map/all_to_all | solution.py:89
  168.3 33.8 %all_gather.7 = bf16[8,2,2048]{0,1,2:T(2,128)(2,1)S(1)} all-gather(bf16[8,2,64]{0,1,2:T(2,128)(2,1)S(1)} %bitcast.278), channel_id=1, replica_groups=mesh['mode'=16,'mer'=32] {'mer'}, dimensions={2}, use_global_device_ids=true | all-gather | bytes 67584 | tf_op jit(solution)/shard_map/all_gather | solution.py:102
  205.6 2.2 reshape.400
  226.3 9.4 %all-to-all-start.3 = ((f32[16,1,1536]{2,1,0:T(1,128)}), f32[16,1,1536]{2,1,0:T(1,128)S(1)}, u32[]{:S(2)}, u32[]{:S(2)}) async-start(f32[16,1,1536]{2,1,0:T(1,128)} %reshape.401), calls=%async_computation.3 | async-start | bytes 196608 | tf_op jit(solution)/shard_map/all_to_all | solution.py:92
  237.2 9.1 %all-to-all-done.3 = f32[16,1,1536]{2,1,0:T(1,128)S(1)} async-done(((f32[16,1,1536]{2,1,0:T(1,128)}), f32[16,1,1536]{2,1,0:T(1,128)S(1)}, u32[]{:S(2)}, u32[]{:S(2)}) %all-to-all-start.3) | async-done | bytes 98336 | tf_op jit(solution)/shard_map/all_to_all | solution.py:92
  253.2 9.5 %while.25 = (s32[]{:T(128)}, f32[48,768]{1,0:T(8,128)S(1)}, s32[2,512]{1,0:T(2,128)S(1)}, bf16[96,768]{1,0:T(8,128)(2,1)}, bf16[96,768]{1,0:T(8,128)(2,1)}, /*in...) while((s32[]{:T(128)}, f32[48,768]{1,0:T(8,128)S(1)}, ...), condition=%wide.region_5.6_spmd.clone, body=%wide.region_4.5_spmd.clone.sunk | while | flops 266170368 | bytes 3485803 | solution.py:80
  262.8 3.2 %collective-permute-start.5 = (f32[8,6,256]{2,0,1:T(8,128)S(1)}, f32[8,6,256]{2,0,1:T(8,128)S(1)}, u32[]{:S(2)}, u32[]{:S(2)}) collective-permute-start(f32[8,6,256]{2,0,1:T(8,128)S(1)} %copy.258), channel_id=1, source_target_pairs={{0,1},{1,2},{2,3},{3,4},{4,5},{5,6},{6,7},{7,8},{8,9},{9,10},{10,1... | collective-permute-start | bytes 147464 | tf_op jit(solution)/shard_map/ppermute | solution.py:13
  266.9 3.5 %collective-permute-done.5 = f32[8,6,256]{2,0,1:T(8,128)S(1)} collective-permute-done((f32[8,6,256]{2,0,1:T(8,128)S(1)}, f32[8,6,256]{2,0,1:T(8,128)S(1)}, u32[]{:S(2)}, u32[]{:S(2)}) %collective-permute-start.5) | collective-permute-done | bytes 49184 | tf_op jit(solution)/shard_map/ppermute | solution.py:13
  272.1 7.0 %scatter_fusion.2 = f32[8,6,512]{0,2,1:T(8,128)} fusion(f32[8,6,512]{0,2,1:T(8,128)} %copy.261, s32[64]{0:T(128)S(1)} %select_bitcast_fusion.1, f32[64,8]{1,0:T(8,128)S(1)} %copy.262), kind=kCustom, calls=%fused_computation.6 | custom fusion | flops 512 | bytes 6656 | tf_op jit(solution)/shard_map/scatter-add | solution.py:107
  279.1 7.0 %scatter_fusion.3 = f32[8,6,512]{0,2,1:T(8,128)} fusion(f32[8,6,512]{0,2,1:T(8,128)} %scatter_fusion.2, s32[64]{0:T(128)S(1)} %get-tuple-element.204, f32[64,8]{1,0:T(8,128)S(1)} %copy.263), kind=kCustom, calls=%fused_computation.7 | custom fusion | flops 512 | bytes 6656 | tf_op jit(solution)/shard_map/scatter-add | solution.py:108
  (267 shorter events, 106.1 us)
Async XLA Ops:
  0.6 59.4 %copy-start = (bf16[8,64,2048]{2,1,0:T(8,128)(2,1)S(1)}, bf16[8,64,2048]{2,1,0:T(8,128)(2,1)}, u32[]{:S(2)}) copy-start(bf16[8,64,2048]{2,1,0:T(8,128)(2,1)} %param.25) | copy-start | bytes 6291460
  3.6 15.9 %copy-start.3 = (f32[8,6,512]{2,0,1:T(8,128)S(1)}, f32[8,6,512]{2,0,1:T(8,128)}, u32[]{:S(2)}) copy-start(f32[8,6,512]{2,0,1:T(8,128)} %param.18) | copy-start | bytes 294916
  3.6 19.5 %copy-start.13 = (bf16[3,256,32]{1,2,0:T(8,128)(2,1)S(1)}, bf16[3,256,32]{1,2,0:T(8,128)(2,1)}, u32[]{:S(2)}) copy-start(bf16[3,256,32]{1,2,0:T(8,128)(2,1)} %param.19) | copy-start | bytes 147460
  3.7 20.0 %copy-start.25 = (s32[64]{0:T(128)S(1)}, s32[64]{0:T(128)}, u32[]{:S(2)}) copy-start(s32[64]{0:T(128)} %param.24) | copy-start | bytes 772
  3.7 20.0 %copy-start.24 = (s32[2]{0:T(128)S(1)}, s32[2]{0:T(128)}, u32[]{:S(2)}) copy-start(s32[2]{0:T(128)} %constant.185) | copy-start | bytes 28
  6.6 54.6 %all-to-all-start = ((f32[16,1,1536]{2,1,0:T(1,128)}), f32[16,1,1536]{2,1,0:T(1,128)}, u32[]{:S(2)}, u32[]{:S(2)}) async-start(f32[16,1,1536]{2,1,0:T(1,128)} %reshape.395), calls=%async_computation | async-start | bytes 196608 | tf_op jit(solution)/shard_map/all_to_all | solution.py:89
  20.2 94.5 %collective-permute-start = (f32[8,6,256]{2,0,1:T(8,128)}, f32[8,6,256]{2,0,1:T(8,128)}, u32[]{:S(2)}, u32[]{:S(2)}) collective-permute-start(f32[8,6,256]{2,0,1:T(8,128)} %slice.192), channel_id=1, source_target_pairs={{1,0},{2,1},{3,2},{4,3},{5,4},{6,5},{7,6},{8,7},{9,8},{10,9},{11,1... | collective-permute-start | bytes 147464 | tf_op jit(solution)/shard_map/ppermute | solution.py:13
  23.1 45.6 %copy-start.8 = (f32[3,256,32]{1,2,0:T(8,128)}, f32[3,256,32]{1,2,0:T(8,128)S(1)}, u32[]{:S(2)}) copy-start(f32[3,256,32]{1,2,0:T(8,128)S(1)} %convert_element_type.56) | copy-start | bytes 294916
  60.7 53.8 %copy-start.14 = (f32[8,2,64]{2,1,0:T(2,128)}, f32[8,2,64]{2,1,0:T(2,128)S(1)}, u32[]{:S(2)}) copy-start(f32[8,2,64]{2,1,0:T(2,128)S(1)} %fusion.71) | copy-start | bytes 12292
  73.4 27.4 %copy-start.16 = (f32[512]{0:T(512)S(1)}, f32[512]{0:T(512)}, u32[]{:S(2)}) copy-start(f32[512]{0:T(512)} %param.22) | copy-start | bytes 6148
  91.0 23.5 %copy-start.18 = (s32[16,64]{1,0:T(8,128)S(1)}, s32[16,64]{1,0:T(8,128)}, u32[]{:S(2)}) copy-start(s32[16,64]{1,0:T(8,128)} %param.23) | copy-start | bytes 12292
  91.0 25.2 %copy-start.4 = (f32[8,6,512]{2,0,1:T(8,128)S(1)}, f32[8,6,512]{2,0,1:T(8,128)}, u32[]{:S(2)}) copy-start(f32[8,6,512]{2,0,1:T(8,128)} %param.18) | copy-start | bytes 294916
  91.0 20.1 %all-to-all-start.1 = ((f32[16,1,1536]{2,1,0:T(1,128)}), f32[16,1,1536]{2,1,0:T(1,128)S(1)}, u32[]{:S(2)}, u32[]{:S(2)}) async-start(f32[16,1,1536]{2,1,0:T(1,128)} %reshape.397), calls=%async_computation.1 | async-start | bytes 196608 | tf_op jit(solution)/shard_map/all_to_all | solution.py:92
  112.6 3.7 %collective-permute-start.1 = (f32[8,6,256]{2,0,1:T(8,128)S(1)}, f32[8,6,256]{2,0,1:T(8,128)S(1)}, u32[]{:S(2)}, u32[]{:S(2)}) collective-permute-start(f32[8,6,256]{2,0,1:T(8,128)S(1)} %slice.245), channel_id=1, source_target_pairs={{1,0},{2,1},{3,2},{4,3},{5,4},{6,5},{7,6},{8,7},{9,8},{10,9},{11,1... | collective-permute-start | bytes 147464 | tf_op jit(solution)/shard_map/ppermute | solution.py:13
  118.0 14.9 %copy-start.23 = (s32[64]{0:T(128)S(1)}, s32[64]{0:T(128)}, u32[]{:S(2)}) copy-start(s32[64]{0:T(128)} %copy-done.22) | copy-start | bytes 772
  129.8 7.5 %collective-permute-start.2 = (f32[8,6,256]{2,0,1:T(8,128)S(1)}, f32[8,6,256]{2,0,1:T(8,128)S(1)}, u32[]{:S(2)}, u32[]{:S(2)}) collective-permute-start(f32[8,6,256]{2,0,1:T(8,128)S(1)} %copy.228), channel_id=1, source_target_pairs={{0,1},{1,2},{2,3},{3,4},{4,5},{5,6},{6,7},{7,8},{8,9},{9,10},{10,1... | collective-permute-start | bytes 147464 | tf_op jit(solution)/shard_map/ppermute | solution.py:13
  137.4 17.6 %copy-start.17 = (f32[512]{0:T(512)S(1)}, f32[512]{0:T(512)}, u32[]{:S(2)}) copy-start(f32[512]{0:T(512)} %param.22) | copy-start | bytes 6148
  159.9 43.8 %all-to-all-start.2 = ((f32[16,1,1536]{2,1,0:T(1,128)}), f32[16,1,1536]{2,1,0:T(1,128)}, u32[]{:S(2)}, u32[]{:S(2)}) async-start(f32[16,1,1536]{2,1,0:T(1,128)} %reshape.399), calls=%async_computation.2 | async-start | bytes 196608 | tf_op jit(solution)/shard_map/all_to_all | solution.py:89
  165.4 84.4 %collective-permute-start.3 = (f32[8,6,256]{2,0,1:T(8,128)}, f32[8,6,256]{2,0,1:T(8,128)}, u32[]{:S(2)}, u32[]{:S(2)}) collective-permute-start(f32[8,6,256]{2,0,1:T(8,128)} %slice.254), channel_id=1, source_target_pairs={{1,0},{2,1},{3,2},{4,3},{5,4},{6,5},{7,6},{8,7},{9,8},{10,9},{11,1... | collective-permute-start | bytes 147464 | tf_op jit(solution)/shard_map/ppermute | solution.py:13
  226.3 20.1 %all-to-all-start.3 = ((f32[16,1,1536]{2,1,0:T(1,128)}), f32[16,1,1536]{2,1,0:T(1,128)S(1)}, u32[]{:S(2)}, u32[]{:S(2)}) async-start(f32[16,1,1536]{2,1,0:T(1,128)} %reshape.401), calls=%async_computation.3 | async-start | bytes 196608 | tf_op jit(solution)/shard_map/all_to_all | solution.py:92
  237.2 14.3 %copy-start.7 = (f32[8,6,512]{2,0,1:T(8,128)S(1)}, f32[8,6,512]{2,0,1:T(8,128)}, u32[]{:S(2)}) copy-start(f32[8,6,512]{2,0,1:T(8,128)} %copy-done.6) | copy-start | bytes 294916
  247.8 3.7 %collective-permute-start.4 = (f32[8,6,256]{2,0,1:T(8,128)S(1)}, f32[8,6,256]{2,0,1:T(8,128)S(1)}, u32[]{:S(2)}, u32[]{:S(2)}) collective-permute-start(f32[8,6,256]{2,0,1:T(8,128)S(1)} %slice.255), channel_id=1, source_target_pairs={{1,0},{2,1},{3,2},{4,3},{5,4},{6,5},{7,6},{8,7},{9,8},{10,9},{11,1... | collective-permute-start | bytes 147464 | tf_op jit(solution)/shard_map/ppermute | solution.py:13
  262.8 7.6 %collective-permute-start.5 = (f32[8,6,256]{2,0,1:T(8,128)S(1)}, f32[8,6,256]{2,0,1:T(8,128)S(1)}, u32[]{:S(2)}, u32[]{:S(2)}) collective-permute-start(f32[8,6,256]{2,0,1:T(8,128)S(1)} %copy.258), channel_id=1, source_target_pairs={{0,1},{1,2},{2,3},{3,4},{4,5},{5,6},{6,7},{7,8},{8,9},{9,10},{10,1... | collective-permute-start | bytes 147464 | tf_op jit(solution)/shard_map/ppermute | solution.py:13
  270.4 17.6 %copy-start.5 = (f32[8,6,512]{2,0,1:T(8,128)S(1)}, f32[8,6,512]{2,0,1:T(8,128)}, u32[]{:S(2)}) copy-start(f32[8,6,512]{2,0,1:T(8,128)} %param.18) | copy-start | bytes 294916
  (14 other events, 50.2 us)
